TPU v7x, 32 devices: a whole 2x2x4 slice. The times are simulated.
32 devices in a mesh: dp: 4 (over z), expert: 8 (over y, x, core).
Axes of the slice: x: 2, y: 2, z: 4, core: 2. Of those that a mesh axis runs over, the one named last changes fastest.
Arguments:
- tokens: bfloat16 [8, 512, 2048], P('expert', 'dp'), may hold values from -12 to 12
- routes: int32 [8, 512, 2], P('expert', 'dp'), may hold values from 0 to 7, all different within a row; in each aligned block of 128 rows (0 to 127, 128 to 255, ..., all dimensions but the last counted through in order) at most 40 rows name the same one
- gate_code: int32 [8, 512, 2], P('expert', 'dp'), may hold values from 0 to 15
- gate_table: float32 [16], replicated, may hold values from 0.1 to 1
- w_gate: bfloat16 [8, 2048, 704], P('expert'), may hold values from -0.125 to 0.125
- w_up: bfloat16 [8, 2048, 704], P('expert'), may hold values from -0.125 to 0.125
- w_down: bfloat16 [8, 704, 2048], P('expert'), may hold values from -0.7 to 0.7
- norm_gain: float32 [2048], replicated, may hold values from 0.25 to 1.75
Outputs:
- relaid_out: bfloat16 [8, 512, 2048], P('expert', None, 'dp')
Inputs may be any that keep to these rules, and one draw needn't show every extreme that they name: Within the 128 tokens of one device (aligned blocks of positions) no expert is named by more than 40 routes, a bound that some block reaches; a token's two experts differ.
All inputs are finite; a program needn't handle non-finite values.
Results may differ from a plain program's by a relative error of at most 0.0064.
Values may be sent and summed in bfloat16 or wider, within the bound.
No kernel may reach another device: no remote copies, remote signals or barrier semaphores. Data moves between devices by JAX's collectives and lax.ppermute only.
A program may use at most 64 MiB of HBM per device.

v0:
```python
import jax
import jax.numpy as jnp
from jax import lax
from jax.sharding import PartitionSpec as P

epsilon = 1e-06


def expert_ffn(slot_block, w_gate, w_up, w_down):
    shape_in = slot_block.shape
    flat_rows = slot_block.reshape(-1, shape_in[-1])
    gate_act = jnp.dot(flat_rows, w_gate[0], preferred_element_type=jnp.float32)
    up_act = jnp.dot(flat_rows, w_up[0], preferred_element_type=jnp.float32)
    hidden = (jax.nn.silu(gate_act) * up_act).astype(jnp.bfloat16)
    result = jnp.dot(hidden, w_down[0], preferred_element_type=jnp.float32).astype(jnp.bfloat16)
    return result.reshape(shape_in)


def lookup(codes, gate_table):
    levels = gate_table.shape[0]
    match = codes[:, None] == jnp.arange(levels, dtype=jnp.int32)[None, :]
    return jnp.sum(jnp.where(match, gate_table[None, :], 0.0), axis=1)


def combine_pairs(outputs, weights):
    combined = outputs[:, 0] * weights[:, 0:1] + outputs[:, 1] * weights[:, 1:2]
    rounded = lax.optimization_barrier(combined.astype(jnp.bfloat16))
    return rounded.astype(jnp.float32)


def local(tokens, routes, gate_code, gate_table, w_gate, w_up, w_down, norm_gain):
    own_rows = tokens[0]
    tok_count, feat_width = own_rows.shape
    experts = w_gate.shape[0] * lax.axis_size("expert")
    capacity = 5 * tok_count // (2 * experts)
    route_ids = routes[0].reshape(-1)
    onehot = (route_ids[:, None] == jnp.arange(experts, dtype=jnp.int32)[None, :]).astype(jnp.int32)
    slot_pos = jnp.sum((jnp.cumsum(onehot, axis=0) - onehot) * onehot, axis=1)
    position = route_ids * capacity + slot_pos
    owner_row = (
        jnp.zeros((experts * capacity,), jnp.int32)
        .at[position]
        .set(jnp.arange(2 * tok_count, dtype=jnp.int32) // 2)
    )
    filled = jnp.zeros((experts * capacity,), jnp.bool_).at[position].set(True)
    buffer = jnp.where(filled[:, None], own_rows[owner_row], jnp.zeros((), jnp.bfloat16))
    buffer = buffer.reshape(experts, capacity, feat_width)
    level_ids = gate_code[0].reshape(-1)
    received = lax.all_to_all(buffer, "expert", split_axis=0, concat_axis=0, tiled=True)
    expert_out = expert_ffn(received, w_gate, w_up, w_down)
    returned = lax.all_to_all(expert_out, "expert", split_axis=0, concat_axis=0, tiled=True)
    outputs = (
        returned.reshape(-1, feat_width)[position]
        .astype(jnp.float32)
        .reshape(tok_count, 2, feat_width)
    )
    weights = lookup(level_ids, gate_table).reshape(tok_count, 2)
    widened = combine_pairs(outputs, weights)
    inv_rms = lax.rsqrt(jnp.mean(widened * widened, axis=1, keepdims=True) + epsilon)
    normed = (widened * inv_rms * norm_gain[None, :]).astype(jnp.bfloat16)
    relaid = lax.all_to_all(normed, "dp", split_axis=1, concat_axis=0, tiled=True)
    return relaid[None]


def solution(mesh):
    in_specs = (
        P("expert", "dp", None),
        P("expert", "dp", None),
        P("expert", "dp", None),
        P(),
        P("expert", None, None),
        P("expert", None, None),
        P("expert", None, None),
        P(),
    )
    out_specs = P("expert", None, "dp")
    return jax.shard_map(local, mesh=mesh, in_specs=in_specs, out_specs=out_specs, check_vma=False)
```

profile of v0, /device:TPU:2, one launch (start us, length us, event | category | flops | bytes accessed | tf_op | source)
XLA Modules:
  0.0 100.8 jit_solution(10024853014143610538)
XLA Ops:
  0.0 0.0 copy-start
  0.0 0.9 copy.24
  0.9 0.1 eq.44
  1.1 0.1 eq.40
  1.2 0.7 broadcast_multiply_fusion
  1.9 0.6 reduce-window.6
  2.5 0.2 slice_reduce_fusion.2
  2.8 0.1 copy.23
  2.9 0.1 mul.67
  3.0 0.1 fusion.25
  3.1 1.4 %scatter_custom_fusion.1 = s32[320]{0:T(512)S(1)} fusion(s32[256]{0:T(256)S(1)} %bitcast.61, s32[256]{0:T(256)S(1)} %and_select_fusion, s32[]{:T(128)} %constant.34.clone.1), kind=kCustom, calls=%fused_computation.45 | custom fusion | bytes 1284 | tf_op jit(solution)/shard_map/scatter | solution.py:43
  4.6 1.5 %scatter_custom_fusion = pred[320]{0:T(512)(128)(4,1)S(1)} fusion(s32[256]{0:T(256)S(1)} %bitcast.62, pred[256]{0:T(512)(128)(4,1)S(1)} %broadcast.79, pred[]{:T(512)} %constant.16.clone.1), kind=kCustom, calls=%fused_computation.47 | custom fusion | bytes 321 | tf_op jit(solution)/shard_map/scatter | solution.py:45
  6.0 0.1 broadcast_in_dim.49
  6.1 6.1 %gather_fusion = bf16[320,2048]{1,0:T(8,128)(2,1)} fusion(bf16[128,2048]{1,0:T(8,128)(2,1)} %bitcast.53, s32[1024]{0:T(1024)S(1)} %pad_clamp_fusion.1), kind=kCustom, calls=%fused_computation | custom fusion | bytes 2622720 | tf_op jit(solution)/shard_map/gather | solution.py:46
  12.2 0.0 copy-start.5
  12.2 1.6 %broadcast_select_fusion = bf16[8,40,2048]{2,1,0:T(8,128)(2,1)S(1)} fusion(bf16[8,40,2048]{2,1,0:T(8,128)(2,1)} %bitcast.54, pred[8,40]{1,0:T(8,128)(4,1)S(1)} %broadcast_in_dim.49), kind=kLoop, calls=%fused_computation.14 | loop fusion | flops 655360 | bytes 2621760 | tf_op jit(solution)/shard_map/jit(_where)/select_n | solution.py:46
  13.9 20.7 %all_to_all.26 = bf16[8,40,2048]{2,1,0:T(8,128)(2,1)S(1)} all-to-all(bf16[8,40,2048]{2,1,0:T(8,128)(2,1)S(1)} %broadcast_select_fusion), channel_id=1, replica_groups=mesh['dp'=4,'expert'=8] {'expert'}, dimensions={0} | all-to-all | bytes 2621440 | tf_op jit(solution)/shard_map/all_to_all | solution.py:49
  34.6 0.0 copy-start.1
  34.6 1.1 %copy-done.1 = bf16[8,40,2048]{2,1,0:T(8,128)(2,1)} copy-done((bf16[8,40,2048]{2,1,0:T(8,128)(2,1)}, bf16[8,40,2048]{2,1,0:T(8,128)(2,1)S(1)}, u32[]{:S(2)}) %copy-start.1) | copy-done | bytes 1310744
  35.7 0.0 copy-done.5
  35.7 2.2 %fusion.4 = f32[320,704]{1,0:T(8,128)} fusion(bf16[320,2048]{1,0:T(8,128)(2,1)S(1)} %bitcast.59, bf16[1,2048,704]{1,2,0:T(8,128)(2,1)S(1)} %copy-done.5), kind=kOutput, calls=%fused_computation.8 | convolution fusion | flops 922746880 | bytes 5095424 | tf_op jit(solution)/shard_map/dot_general | solution.py:12
  37.9 0.0 copy-done
  37.9 6.1 %fusion.6 = bf16[320,2048]{1,0:T(8,128)(2,1)} fusion(bf16[1,704,2048]{2,1,0:T(8,128)(2,1)S(1)} %copy-done, bf16[320,2048]{1,0:T(8,128)(2,1)} %bitcast.60, bf16[1,2048,704]{1,2,0:T(8,128)(2,1)} %param.13, f32[320,704]{1,0:T(8,128)} %fusion.4), kind=kOutput, calls=%fused_computation.10 | convolution fusion | flops 1847500800 | bytes 9289728 | tf_op jit(solution)/shard_map/dot_general | solution.py:15
  44.0 0.0 copy-start.3
  44.0 0.0 copy-start.4
  44.0 5.7 %all-to-all-start.1 = ((bf16[8,40,2048]{2,1,0:T(8,128)(2,1)}), bf16[8,40,2048]{2,1,0:T(8,128)(2,1)}, u32[]{:S(2)}, u32[]{:S(2)}) async-start(bf16[8,40,2048]{2,1,0:T(8,128)(2,1)} %bitcast.58), calls=%async_computation.1 | async-start | bytes 2621440 | tf_op jit(solution)/shard_map/all_to_all | solution.py:51
  49.8 0.0 copy-done.3
  49.8 0.1 copy.27
  49.9 0.1 eq.48
  50.0 0.0 copy-done.4
  50.0 0.1 select_reduce_fusion
  50.1 0.1 reshape.88
  50.3 0.2 slice_reduce_fusion.1
  50.5 16.1 %all-to-all-done.1 = bf16[8,40,2048]{2,1,0:T(8,128)(2,1)} async-done(((bf16[8,40,2048]{2,1,0:T(8,128)(2,1)}), bf16[8,40,2048]{2,1,0:T(8,128)(2,1)}, u32[]{:S(2)}, u32[]{:S(2)}) %all-to-all-start.1) | async-done | bytes 1310752 | tf_op jit(solution)/shard_map/all_to_all | solution.py:51
  66.6 4.8 %gather_fusion.1 = bf16[256,2048]{1,0:T(8,128)(2,1)} fusion(bf16[320,2048]{1,0:T(8,128)(2,1)} %bitcast.11, s32[1024]{0:T(1024)S(1)} %pad_clamp_fusion), kind=kCustom, calls=%fused_computation.1 | custom fusion | bytes 2098176 | tf_op jit(solution)/shard_map/gather | solution.py:53
  71.4 3.3 %reshape.89 = f32[128,2,2048]{2,1,0:T(2,128)} reshape(bf16[256,2048]{1,0:T(8,128)(2,1)} %gather_fusion.1) | data formatting | bytes 3145728 | tf_op jit(solution)/shard_map/convert_element_type | solution.py:54
  74.8 4.4 %fusion.32 = (f32[128,1,2048]{2,1,0:T(1,128)S(1)}, f32[128,1,2048]{2,1,0:T(1,128)S(1)}) fusion(f32[128,2,2048]{2,1,0:T(2,128)} %reshape.89), kind=kLoop, calls=%fused_computation.52 | loop fusion | bytes 4194304 | tf_op jit(solution)/shard_map/slice | solution.py:26
  79.1 0.0 copy-start.2
  79.2 1.0 %fusion.20 = bf16[128,2048]{1,0:T(8,128)(2,1)S(1)} fusion(f32[128,1,2048]{2,1,0:T(1,128)S(1)} %get-tuple-element.8, f32[128,1,2048]{2,1,0:T(1,128)S(1)} %get-tuple-element.7, f32[128]{0:T(128)S(1)} %get-tuple-element.6, f32[128]{0:T(128)S(1)} %get-tuple-element.5), kind=kLoop, calls=%fused_computation.22 | loop fusion | flops 1048576 | bytes 2622464 | tf_op jit(solution)/shard_map/convert_element_type | solution.py:27
  80.2 0.2 fusion.15
  80.4 0.0 copy-done.2
  80.4 0.2 fusion.17
  80.6 19.4 %all_to_all.27 = bf16[128,4,512]{2,0,1:T(8,128)(2,1)S(1)} all-to-all(bf16[128,4,512]{2,0,1:T(8,128)(2,1)S(1)} %bitcast.56), channel_id=1, replica_groups=mesh['dp'=4,'expert'=8] {'dp'}, dimensions={1} | all-to-all | bytes 1048576 | tf_op jit(solution)/shard_map/all_to_all | solution.py:61
  100.0 0.8 copy.43
  (11 shorter events, 0.1 us)
Async XLA Ops:
  0.0 37.9 %copy-start = (bf16[1,704,2048]{2,1,0:T(8,128)(2,1)S(1)}, bf16[1,704,2048]{2,1,0:T(8,128)(2,1)}, u32[]{:S(2)}) copy-start(bf16[1,704,2048]{2,1,0:T(8,128)(2,1)} %param.14) | copy-start | bytes 8650756
  12.2 23.4 %copy-start.5 = (bf16[1,2048,704]{1,2,0:T(8,128)(2,1)S(1)}, bf16[1,2048,704]{1,2,0:T(8,128)(2,1)}, u32[]{:S(2)}) copy-start(bf16[1,2048,704]{1,2,0:T(8,128)(2,1)} %param.12) | copy-start | bytes 8650756
  34.6 1.1 %copy-start.1 = (bf16[8,40,2048]{2,1,0:T(8,128)(2,1)}, bf16[8,40,2048]{2,1,0:T(8,128)(2,1)S(1)}, u32[]{:S(2)}) copy-start(bf16[8,40,2048]{2,1,0:T(8,128)(2,1)S(1)} %all_to_all.26) | copy-start | bytes 3932164
  44.0 5.8 %copy-start.3 = (s32[1,128,2]{1,2,0:T(2,128)S(1)}, s32[1,128,2]{1,2,0:T(2,128)}, u32[]{:S(2)}) copy-start(s32[1,128,2]{1,2,0:T(2,128)} %param.10) | copy-start | bytes 3076
  44.0 6.0 %copy-start.4 = (f32[16]{0:T(128)S(1)}, f32[16]{0:T(128)}, u32[]{:S(2)}) copy-start(f32[16]{0:T(128)} %param.11) | copy-start | bytes 196
  44.0 22.5 %all-to-all-start.1 = ((bf16[8,40,2048]{2,1,0:T(8,128)(2,1)}), bf16[8,40,2048]{2,1,0:T(8,128)(2,1)}, u32[]{:S(2)}, u32[]{:S(2)}) async-start(bf16[8,40,2048]{2,1,0:T(8,128)(2,1)} %bitcast.58), calls=%async_computation.1 | async-start | bytes 2621440 | tf_op jit(solution)/shard_map/all_to_all | solution.py:51
  79.1 1.2 %copy-start.2 = (f32[2048]{0:T(1024)S(1)}, f32[2048]{0:T(1024)}, u32[]{:S(2)}) copy-start(f32[2048]{0:T(1024)} %param.15) | copy-start | bytes 24580
where the time goes:
time: 101 us
  blocking collectives  40.1 us (40%)
  local copies, waits for them, and re-layouts  25.8 us (26%)
  waiting for transfers between devices  16.1 us (16%)
  matrix products  8.36 us (8%)
  starting transfers between devices  5.75 us (6%)
  other arithmetic  4.54 us (4%)
    all_to_all x1, blocking collectives, local(): lax.all_to_all(buffer, 'expert', split_axis=0, concat_axis=0, tiled=True)  20.7 us
    all_to_all x1, blocking collectives, local(): lax.all_to_all(normed, 'dp', split_axis=1, concat_axis=0, tiled=True)  19.4 us
    all_to_all x1, waiting for transfers between devices, local(): lax.all_to_all(expert_out, 'expert', split_axis=0, concat_axis=0, tiled=T...  16.1 us
    dot_general x1, matrix products, expert_ffn(): jnp.dot(hidden, w_down[0], preferred_element_type=jnp.float32)  6.15 us
    gather x1, local copies, waits for them, and re-layouts, local(): own_rows[owner_row]  6.09 us
    all_to_all x1, starting transfers between devices, local(): lax.all_to_all(expert_out, 'expert', split_axis=0, concat_axis=0, tiled=T...  5.75 us
    gather x1, local copies, waits for them, and re-layouts, local(): returned.reshape(-1, feat_width)[position].astype(jnp.float32)  4.84 us
    slice x2, local copies, waits for them, and re-layouts, combine_pairs(): combined = outputs[:, 0] * weights[:, 0:1] + outputs[:, 1] * weights[:, 1:2]  4.55 us
  transfers between devices with their start and end apart: 1, of which 1 were waited for; matrix products, arithmetic and copies ran while one was open for 1% of the time, Pallas kernels for 0%

commit v1 on v0

--- a/solution.py
+++ b/solution.py
@@ -58,7 +58,10 @@
     widened = combine_pairs(outputs, weights)
     inv_rms = lax.rsqrt(jnp.mean(widened * widened, axis=1, keepdims=True) + epsilon)
     normed = (widened * inv_rms * norm_gain[None, :]).astype(jnp.bfloat16)
-    relaid = lax.all_to_all(normed, "dp", split_axis=1, concat_axis=0, tiled=True)
+    size = lax.axis_size("dp")
+    pieces = jnp.stack(jnp.split(normed, size, axis=1), axis=0)
+    pieces = lax.all_to_all(pieces, "dp", split_axis=0, concat_axis=0)
+    relaid = jnp.concatenate(pieces, axis=0)
     return relaid[None]
 
 

time: 101 us -> 101 us (level)
  no operation moved by 1% of the time
where the time goes in v1:
time: 101 us
  blocking collectives  40.1 us (40%)
  local copies, waits for them, and re-layouts  25.8 us (26%)
  waiting for transfers between devices  16.1 us (16%)
  matrix products  8.36 us (8%)
  starting transfers between devices  5.75 us (6%)
  other arithmetic  4.61 us (5%)
    all_to_all x1, blocking collectives, local(): lax.all_to_all(buffer, 'expert', split_axis=0, concat_axis=0, tiled=True)  20.7 us
    all_to_all x1, blocking collectives, local(): pieces = lax.all_to_all(pieces, 'dp', split_axis=0, concat_axis=0)  19.4 us
    all_to_all x1, waiting for transfers between devices, local(): lax.all_to_all(expert_out, 'expert', split_axis=0, concat_axis=0, tiled=T...  16.1 us
    dot_general x1, matrix products, expert_ffn(): jnp.dot(hidden, w_down[0], preferred_element_type=jnp.float32)  6.15 us
    gather x1, local copies, waits for them, and re-layouts, local(): own_rows[owner_row]  6.09 us
    all_to_all x1, starting transfers between devices, local(): lax.all_to_all(expert_out, 'expert', split_axis=0, concat_axis=0, tiled=T...  5.75 us
    gather x1, local copies, waits for them, and re-layouts, local(): returned.reshape(-1, feat_width)[position].astype(jnp.float32)  4.84 us
    slice x2, local copies, waits for them, and re-layouts, combine_pairs(): combined = outputs[:, 0] * weights[:, 0:1] + outputs[:, 1] * weights[:, 1:2]  4.55 us
  transfers between devices with their start and end apart: 1, of which 1 were waited for; matrix products, arithmetic and copies ran while one was open for 1% of the time, Pallas kernels for 0%

profile of v1, /device:TPU:2, one launch (start us, length us, event | category | flops | bytes accessed | tf_op | source)
XLA Modules:
  0.0 100.9 jit_solution(5468148255370982929)
XLA Ops:
  0.0 0.0 copy-start
  0.0 0.9 copy.21
  0.9 0.1 eq.44
  1.1 0.1 eq.40
  1.2 0.7 broadcast_multiply_fusion
  1.9 0.6 reduce-window.6
  2.5 0.2 slice_reduce_fusion.2
  2.8 0.1 copy.20
  2.9 0.1 mul.67
  3.0 0.1 fusion.25
  3.1 1.4 %scatter_custom_fusion.1 = s32[320]{0:T(512)S(1)} fusion(s32[256]{0:T(256)S(1)} %bitcast.61, s32[256]{0:T(256)S(1)} %and_select_fusion, s32[]{:T(128)} %constant.34.clone.1), kind=kCustom, calls=%fused_computation.49 | custom fusion | bytes 1284 | tf_op jit(solution)/shard_map/scatter | solution.py:43
  4.6 1.5 %scatter_custom_fusion = pred[320]{0:T(512)(128)(4,1)S(1)} fusion(s32[256]{0:T(256)S(1)} %bitcast.62, pred[256]{0:T(512)(128)(4,1)S(1)} %broadcast.79, pred[]{:T(512)} %constant.16.clone.1), kind=kCustom, calls=%fused_computation.51 | custom fusion | bytes 321 | tf_op jit(solution)/shard_map/scatter | solution.py:45
  6.0 0.1 broadcast_in_dim.46
  6.1 6.1 %gather_fusion = bf16[320,2048]{1,0:T(8,128)(2,1)} fusion(bf16[128,2048]{1,0:T(8,128)(2,1)} %bitcast.55, s32[1024]{0:T(1024)S(1)} %pad_clamp_fusion.1), kind=kCustom, calls=%fused_computation | custom fusion | bytes 2622720 | tf_op jit(solution)/shard_map/gather | solution.py:46
  12.2 0.0 copy-start.5
  12.2 1.6 %broadcast_select_fusion = bf16[8,40,2048]{2,1,0:T(8,128)(2,1)S(1)} fusion(bf16[8,40,2048]{2,1,0:T(8,128)(2,1)} %bitcast.56, pred[8,40]{1,0:T(8,128)(4,1)S(1)} %broadcast_in_dim.46), kind=kLoop, calls=%fused_computation.14 | loop fusion | flops 655360 | bytes 2621760 | tf_op jit(solution)/shard_map/jit(_where)/select_n | solution.py:46
  13.9 20.7 %all_to_all.15 = bf16[8,40,2048]{2,1,0:T(8,128)(2,1)S(1)} all-to-all(bf16[8,40,2048]{2,1,0:T(8,128)(2,1)S(1)} %broadcast_select_fusion), channel_id=1, replica_groups=mesh['dp'=4,'expert'=8] {'expert'}, dimensions={0} | all-to-all | bytes 2621440 | tf_op jit(solution)/shard_map/all_to_all | solution.py:49
  34.6 0.0 copy-start.1
  34.6 1.1 %copy-done.1 = bf16[8,40,2048]{2,1,0:T(8,128)(2,1)} copy-done((bf16[8,40,2048]{2,1,0:T(8,128)(2,1)}, bf16[8,40,2048]{2,1,0:T(8,128)(2,1)S(1)}, u32[]{:S(2)}) %copy-start.1) | copy-done | bytes 1310744
  35.7 0.0 copy-done.5
  35.7 2.2 %fusion.4 = f32[320,704]{1,0:T(8,128)} fusion(bf16[320,2048]{1,0:T(8,128)(2,1)S(1)} %bitcast.59, bf16[1,2048,704]{1,2,0:T(8,128)(2,1)S(1)} %copy-done.5), kind=kOutput, calls=%fused_computation.8 | convolution fusion | flops 922746880 | bytes 5095424 | tf_op jit(solution)/shard_map/dot_general | solution.py:12
  37.9 0.0 copy-done
  37.9 6.1 %fusion.6 = bf16[320,2048]{1,0:T(8,128)(2,1)} fusion(bf16[1,704,2048]{2,1,0:T(8,128)(2,1)S(1)} %copy-done, bf16[320,2048]{1,0:T(8,128)(2,1)} %bitcast.60, bf16[1,2048,704]{1,2,0:T(8,128)(2,1)} %param.13, f32[320,704]{1,0:T(8,128)} %fusion.4), kind=kOutput, calls=%fused_computation.10 | convolution fusion | flops 1847500800 | bytes 9289728 | tf_op jit(solution)/shard_map/dot_general | solution.py:15
  44.0 0.0 copy-start.3
  44.0 0.0 copy-start.4
  44.0 5.7 %all-to-all-start.1 = ((bf16[8,40,2048]{2,1,0:T(8,128)(2,1)}), bf16[8,40,2048]{2,1,0:T(8,128)(2,1)}, u32[]{:S(2)}, u32[]{:S(2)}) async-start(bf16[8,40,2048]{2,1,0:T(8,128)(2,1)} %bitcast.58), calls=%async_computation.1 | async-start | bytes 2621440 | tf_op jit(solution)/shard_map/all_to_all | solution.py:51
  49.8 0.0 copy-done.3
  49.8 0.1 copy.24
  49.9 0.1 eq.48
  50.0 0.0 copy-done.4
  50.0 0.1 select_reduce_fusion
  50.1 0.1 reshape.84
  50.3 0.2 slice_reduce_fusion.1
  50.5 16.1 %all-to-all-done.1 = bf16[8,40,2048]{2,1,0:T(8,128)(2,1)} async-done(((bf16[8,40,2048]{2,1,0:T(8,128)(2,1)}), bf16[8,40,2048]{2,1,0:T(8,128)(2,1)}, u32[]{:S(2)}, u32[]{:S(2)}) %all-to-all-start.1) | async-done | bytes 1310752 | tf_op jit(solution)/shard_map/all_to_all | solution.py:51
  66.6 4.8 %gather_fusion.1 = bf16[256,2048]{1,0:T(8,128)(2,1)} fusion(bf16[320,2048]{1,0:T(8,128)(2,1)} %bitcast.11, s32[1024]{0:T(1024)S(1)} %pad_clamp_fusion), kind=kCustom, calls=%fused_computation.1 | custom fusion | bytes 2098176 | tf_op jit(solution)/shard_map/gather | solution.py:53
  71.4 3.3 %reshape.85 = f32[128,2,2048]{2,1,0:T(2,128)} reshape(bf16[256,2048]{1,0:T(8,128)(2,1)} %gather_fusion.1) | data formatting | bytes 3145728 | tf_op jit(solution)/shard_map/convert_element_type | solution.py:54
  74.8 4.4 %fusion.32 = (f32[128,1,2048]{2,1,0:T(1,128)S(1)}, f32[128,1,2048]{2,1,0:T(1,128)S(1)}) fusion(f32[128,2,2048]{2,1,0:T(2,128)} %reshape.85), kind=kLoop, calls=%fused_computation.56 | loop fusion | bytes 4194304 | tf_op jit(solution)/shard_map/slice | solution.py:26
  79.1 0.0 copy-start.2
  79.2 1.0 %fusion.20 = bf16[128,2048]{1,0:T(8,128)(2,1)S(1)} fusion(f32[128,1,2048]{2,1,0:T(1,128)S(1)} %get-tuple-element.8, f32[128,1,2048]{2,1,0:T(1,128)S(1)} %get-tuple-element.7, f32[128]{0:T(128)S(1)} %get-tuple-element.6, f32[128]{0:T(128)S(1)} %get-tuple-element.5), kind=kLoop, calls=%fused_computation.22 | loop fusion | flops 1048576 | bytes 2622464 | tf_op jit(solution)/shard_map/convert_element_type | solution.py:27
  80.2 0.2 fusion.15
  80.4 0.0 copy-done.2
  80.4 0.2 fusion.17
  80.6 0.1 pad_maximum_fusion
  80.7 19.4 %all_to_all.16 = bf16[4,128,512]{2,1,0:T(8,128)(2,1)S(1)} all-to-all(bf16[4,128,512]{2,1,0:T(8,128)(2,1)S(1)} %pad_maximum_fusion), channel_id=1, replica_groups=mesh['dp'=4,'expert'=8] {'dp'}, dimensions={0} | all-to-all | bytes 1048576 | tf_op jit(solution)/shard_map/all_to_all | solution.py:63
  100.1 0.8 copy.36
  (11 shorter events, 0.1 us)
Async XLA Ops:
  0.0 37.9 %copy-start = (bf16[1,704,2048]{2,1,0:T(8,128)(2,1)S(1)}, bf16[1,704,2048]{2,1,0:T(8,128)(2,1)}, u32[]{:S(2)}) copy-start(bf16[1,704,2048]{2,1,0:T(8,128)(2,1)} %param.14) | copy-start | bytes 8650756
  12.2 23.4 %copy-start.5 = (bf16[1,2048,704]{1,2,0:T(8,128)(2,1)S(1)}, bf16[1,2048,704]{1,2,0:T(8,128)(2,1)}, u32[]{:S(2)}) copy-start(bf16[1,2048,704]{1,2,0:T(8,128)(2,1)} %param.12) | copy-start | bytes 8650756
  34.6 1.1 %copy-start.1 = (bf16[8,40,2048]{2,1,0:T(8,128)(2,1)}, bf16[8,40,2048]{2,1,0:T(8,128)(2,1)S(1)}, u32[]{:S(2)}) copy-start(bf16[8,40,2048]{2,1,0:T(8,128)(2,1)S(1)} %all_to_all.15) | copy-start | bytes 3932164
  44.0 5.8 %copy-start.3 = (s32[1,128,2]{1,2,0:T(2,128)S(1)}, s32[1,128,2]{1,2,0:T(2,128)}, u32[]{:S(2)}) copy-start(s32[1,128,2]{1,2,0:T(2,128)} %param.10) | copy-start | bytes 3076
  44.0 6.0 %copy-start.4 = (f32[16]{0:T(128)S(1)}, f32[16]{0:T(128)}, u32[]{:S(2)}) copy-start(f32[16]{0:T(128)} %param.11) | copy-start | bytes 196
  44.0 22.5 %all-to-all-start.1 = ((bf16[8,40,2048]{2,1,0:T(8,128)(2,1)}), bf16[8,40,2048]{2,1,0:T(8,128)(2,1)}, u32[]{:S(2)}, u32[]{:S(2)}) async-start(bf16[8,40,2048]{2,1,0:T(8,128)(2,1)} %bitcast.58), calls=%async_computation.1 | async-start | bytes 2621440 | tf_op jit(solution)/shard_map/all_to_all | solution.py:51
  79.1 1.2 %copy-start.2 = (f32[2048]{0:T(1024)S(1)}, f32[2048]{0:T(1024)}, u32[]{:S(2)}) copy-start(f32[2048]{0:T(1024)} %param.15) | copy-start | bytes 24580
